TPU v7x, 512 devices: a whole 4x4x16 slice. The times are simulated.
512 devices in a mesh: tm: 64 (over y, z), state: 8 (over x, core).
Axes of the slice: x: 4, y: 4, z: 16, core: 2. Of those that a mesh axis runs over, the one named last changes fastest.
Arguments:
- obs: int32 [512], P('tm'), may hold values from 0 to 255
- emit_logits: float32 [256, 2048], P(None, 'state'), may hold values from -0.6 to 0.6
- trans_logits: float32 [16, 3, 128, 128], P('state'), may hold values from -5 to 17
- band_cols: int32 [16, 3], replicated, may hold values from 0 to 15, as said below
- init_logits: float32 [2048], replicated, may hold values from -6 to 6
Outputs:
- posterior: float32 [64, 2048], P('tm', 'state')
Inputs may be any that keep to these rules, and one draw needn't show every extreme that they name: Row r of band_cols names 3 different block columns, the first of them r itself.
All inputs are finite; a program needn't handle non-finite values.
Results may differ from a plain program's by a relative error of at most 0.0006.
The roundings to bfloat16 on the way count: a program that leaves them out, or rounds other values in their place, can miss the bound.
Values may be sent and summed in bfloat16 or wider, within the bound.
A program may use at most 64 MiB of HBM per device.

v0:
```python
import jax
import jax.numpy as jnp
from jax import lax
from jax.sharding import PartitionSpec as P

SEQS = 1
SMOOTH = 0.001


def from_behind(value, axis, steps):
    count = lax.axis_size(axis)
    initial, last = (max(0, -steps), min(count, count - steps))
    return lax.ppermute(value, axis, [(source, source + steps) for source in range(initial, last)])


def form_columns(emit_full, blocks, band_cols, first_col, col_count):
    states = emit_full.shape[1]
    block_count = blocks.shape[0]
    block_size = blocks.shape[2]
    state_rows = jnp.arange(states)[:, None]
    state_cols = first_col + jnp.arange(col_count)[None, :]
    matrix = (state_rows == state_cols).astype(jnp.float32)
    col_scale = jnp.zeros((col_count,), jnp.float32)
    for moment in range(emit_full.shape[0] - 1, -1, -1):
        scaled = (jnp.exp(emit_full[moment])[:, None] * matrix).astype(jnp.bfloat16)
        picked = scaled.reshape(block_count, block_size, col_count)[band_cols]
        product = jnp.einsum(
            "rkij,rkjc->ric", blocks, picked, preferred_element_type=jnp.float32
        ).reshape(states, col_count)
        matrix = product + SMOOTH / states * jnp.sum(scaled, axis=0, dtype=jnp.float32)[None, :]
        col_peak = jnp.max(matrix, axis=0)
        matrix = matrix / col_peak[None, :]
        col_scale = col_scale + jnp.log(col_peak)
    return jnp.log(matrix) + col_scale[None, :]


def on_device(obs, emit_logits, trans_logits, band_cols, init_logits):
    col_count = emit_logits.shape[1]
    state_index = lax.axis_index("state")
    first_col = state_index * col_count
    groups = lax.axis_size("tm") // SEQS
    position = lax.axis_index("tm") % groups
    blocks_own = ((1.0 - SMOOTH) * jax.nn.softmax(trans_logits, axis=(1, 3))).astype(jnp.bfloat16)
    blocks = lax.all_gather(blocks_own, "state", axis=0, tiled=True)
    log_emit = jax.nn.log_softmax(emit_logits, axis=0)
    symbols = emit_logits.shape[0]
    onehot = (obs[:, None] == jnp.arange(symbols)[None, :]).astype(jnp.float32)
    emit_own = jnp.dot(onehot, log_emit, precision=lax.Precision.HIGHEST)
    emit_full = lax.all_gather(emit_own, "state", axis=1, tiled=True)
    own_log = form_columns(emit_full, blocks, band_cols, first_col, col_count)
    left_log = from_behind(own_log, "tm", 1)
    row_peak = lax.pmax(jnp.max(own_log, axis=1), "state")
    peak_own = lax.dynamic_slice_in_dim(row_peak, first_col, col_count)
    shifted = left_log + peak_own[None, :]
    left_peak = lax.pmax(jnp.max(shifted, axis=1), "state")
    weights = jnp.exp(shifted - left_peak[:, None]).astype(jnp.bfloat16)
    right_exp = jnp.exp(own_log - row_peak[:, None]).astype(jnp.bfloat16)
    prior_log = jax.nn.log_softmax(init_logits)
    summed = jnp.dot(
        lax.all_gather(weights, "state", axis=1, tiled=True),
        right_exp,
        preferred_element_type=jnp.float32,
    )
    pair_log = left_peak[:, None] + jnp.log(summed)
    chosen = jnp.where(position == 0, own_log, pair_log)
    col_max = jnp.max(chosen, axis=0)
    scaled_exp = jnp.exp(chosen - col_max[None, :])

    def apply_cols(vector):
        vector_top = jnp.max(vector)
        mixture = jnp.dot(
            jnp.exp(vector - vector_top)[None, :], scaled_exp, precision=lax.Precision.HIGHEST
        )[0]
        return vector_top + col_max + jnp.log(mixture)

    start_cols = apply_cols(prior_log)

    def advance(counter, current):
        incoming = from_behind(current, "tm", 2)
        whole_vector = lax.all_gather(incoming, "state", axis=0, tiled=True)
        return jnp.where(position < 2, start_cols, apply_cols(whole_vector))

    alpha_cols = lax.fori_loop(0, groups // 2 - 1, advance, start_cols)
    vector_top = lax.pmax(jnp.max(alpha_cols), "state")
    total_sum = lax.psum(jnp.sum(jnp.exp(alpha_cols - vector_top)), "state")
    posterior = alpha_cols - vector_top - jnp.log(total_sum)
    return posterior[None, :]


def solution(mesh):
    return jax.shard_map(
        on_device,
        mesh=mesh,
        in_specs=(P("tm"), P(None, "state"), P("state", None, None, None), P(), P()),
        out_specs=P("tm", "state"),
        check_vma=False,
    )
```

profile of v0, /device:TPU:9, one launch (start us, length us, event | category | flops | bytes accessed | tf_op | source)
XLA Modules:
  0.0 896.2 jit_solution(222817929016838769)
XLA Ops:
  13.3 13.6 %all_gather.15 = f32[8,2048]{1,0:T(8,128)S(1)} all-gather(f32[8,256]{1,0:T(8,128)S(1)} %fusion.15), channel_id=1, replica_groups=mesh['tm'=64,'state'=8] {'state'}, dimensions={1}, use_global_device_ids=true | all-gather | bytes 73728 | tf_op jit(solution)/shard_map/all_gather | solution.py:49
  30.6 17.3 %all-gather.6.cloned.1.call-done = bf16[16,3,128,128]{3,2,1,0:T(8,128)(2,1)} async-done(((bf16[2,3,128,128]{3,2,1,0:T(8,128)(2,1)}), bf16[16,3,128,128]{3,2,1,0:T(8,128)(2,1)}) %all-gather.6.cloned.1.call-update) | async-done | bytes 1572880 | tf_op jit(solution)/shard_map/all_gather | solution.py:44
  98.6 12.8 %pmax.21 = f32[2048]{0:T(1024)S(1)} all-reduce(f32[2048]{0:T(1024)S(1)} %bitcast.156), channel_id=1, replica_groups=mesh['tm'=64,'state'=8] {'state'}, use_global_device_ids=true, to_apply=%region_24.25 | all-reduce | flops 2048 | bytes 16384 | tf_op jit(solution)/shard_map/pmax | solution.py:52
  111.5 33.2 %collective-permute-done.1 = f32[2048,256]{1,0:T(8,128)S(1)} collective-permute-done((f32[2048,256]{1,0:T(8,128)}, f32[2048,256]{1,0:T(8,128)S(1)}, u32[]{:S(2)}, u32[]{:S(2)}) %collective-permute-start.1) | collective-permute-done | bytes 2097184 | tf_op jit(solution)/shard_map/ppermute | solution.py:13
  145.1 12.8 %pmax.22 = f32[2048]{0:T(1024)S(1)} all-reduce(f32[2048]{0:T(1024)S(1)} %add_reduce_fusion.1), channel_id=1, replica_groups=mesh['tm'=64,'state'=8] {'state'}, use_global_device_ids=true, to_apply=%region_26.27 | all-reduce | flops 2048 | bytes 16384 | tf_op jit(solution)/shard_map/pmax | solution.py:55
  164.6 54.8 %all-gather.8.cloned.1.call-done = bf16[2048,2048]{1,0:T(8,128)(2,1)} async-done(((bf16[2048,256]{1,0:T(8,128)(2,1)}), bf16[2048,2048]{1,0:T(8,128)(2,1)}) %all-gather.8.cloned.1.call-update) | async-done | bytes 8388624 | tf_op jit(solution)/shard_map/all_gather | solution.py:60
  228.7 630.8 %while.12 = (s32[]{:T(128)}, f32[256]{0:T(256)S(1)}, pred[]{:T(512)}, f32[256]{0:T(256)S(1)}, f32[2048,256]{1,0:T(8,128)S(1)}, /*index=5*/f32[256]{0:T(256)S(1)}, s32[]{:T(128)}, f32[]{:T(128)}) while((s32[]{:T(128)}, f32[256]{0:T(256)S(1)}, pred[]{:T(512)}, f32[256]{0:T(256)S(1)}, f32[2048,256]{1,0:T(8,128)S(1)}, ...), condition=%wide.region_30.31_spmd, body=%wide.region_28.30_spmd.sunk | while | flops 6296321 | bytes 2148494 | solution.py:83
  236.1 11.0 %all-gather.2 = f32[8,1,256]{2,1,0:T(1,128)S(1)} all-gather(f32[1,1,256]{2,1,0:T(1,128)S(1)} %bitcast.157), channel_id=1, replica_groups=mesh['tm'=64,'state'=8] {'state'}, dimensions={0}, use_global_device_ids=true | all-gather | bytes 9216 | tf_op jit(solution)/shard_map/while/body/eval_jaxpr/all_gather | solution.py:80
  276.8 10.9 %all-gather.2 = f32[8,1,256]{2,1,0:T(1,128)S(1)} all-gather(f32[1,1,256]{2,1,0:T(1,128)S(1)} %bitcast.157), channel_id=1, replica_groups=mesh['tm'=64,'state'=8] {'state'}, dimensions={0}, use_global_device_ids=true | all-gather | bytes 9216 | tf_op jit(solution)/shard_map/while/body/eval_jaxpr/all_gather | solution.py:80
  298.1 9.0 %all-gather.2 = f32[8,1,256]{2,1,0:T(1,128)S(1)} all-gather(f32[1,1,256]{2,1,0:T(1,128)S(1)} %bitcast.157), channel_id=1, replica_groups=mesh['tm'=64,'state'=8] {'state'}, dimensions={0}, use_global_device_ids=true | all-gather | bytes 9216 | tf_op jit(solution)/shard_map/while/body/eval_jaxpr/all_gather | solution.py:80
  317.4 10.9 %all-gather.2 = f32[8,1,256]{2,1,0:T(1,128)S(1)} all-gather(f32[1,1,256]{2,1,0:T(1,128)S(1)} %bitcast.157), channel_id=1, replica_groups=mesh['tm'=64,'state'=8] {'state'}, dimensions={0}, use_global_device_ids=true | all-gather | bytes 9216 | tf_op jit(solution)/shard_map/while/body/eval_jaxpr/all_gather | solution.py:80
  338.7 9.0 %all-gather.2 = f32[8,1,256]{2,1,0:T(1,128)S(1)} all-gather(f32[1,1,256]{2,1,0:T(1,128)S(1)} %bitcast.157), channel_id=1, replica_groups=mesh['tm'=64,'state'=8] {'state'}, dimensions={0}, use_global_device_ids=true | all-gather | bytes 9216 | tf_op jit(solution)/shard_map/while/body/eval_jaxpr/all_gather | solution.py:80
  358.1 10.9 %all-gather.2 = f32[8,1,256]{2,1,0:T(1,128)S(1)} all-gather(f32[1,1,256]{2,1,0:T(1,128)S(1)} %bitcast.157), channel_id=1, replica_groups=mesh['tm'=64,'state'=8] {'state'}, dimensions={0}, use_global_device_ids=true | all-gather | bytes 9216 | tf_op jit(solution)/shard_map/while/body/eval_jaxpr/all_gather | solution.py:80
  379.4 9.0 %all-gather.2 = f32[8,1,256]{2,1,0:T(1,128)S(1)} all-gather(f32[1,1,256]{2,1,0:T(1,128)S(1)} %bitcast.157), channel_id=1, replica_groups=mesh['tm'=64,'state'=8] {'state'}, dimensions={0}, use_global_device_ids=true | all-gather | bytes 9216 | tf_op jit(solution)/shard_map/while/body/eval_jaxpr/all_gather | solution.py:80
  398.7 10.9 %all-gather.2 = f32[8,1,256]{2,1,0:T(1,128)S(1)} all-gather(f32[1,1,256]{2,1,0:T(1,128)S(1)} %bitcast.157), channel_id=1, replica_groups=mesh['tm'=64,'state'=8] {'state'}, dimensions={0}, use_global_device_ids=true | all-gather | bytes 9216 | tf_op jit(solution)/shard_map/while/body/eval_jaxpr/all_gather | solution.py:80
  420.0 9.0 %all-gather.2 = f32[8,1,256]{2,1,0:T(1,128)S(1)} all-gather(f32[1,1,256]{2,1,0:T(1,128)S(1)} %bitcast.157), channel_id=1, replica_groups=mesh['tm'=64,'state'=8] {'state'}, dimensions={0}, use_global_device_ids=true | all-gather | bytes 9216 | tf_op jit(solution)/shard_map/while/body/eval_jaxpr/all_gather | solution.py:80
  439.3 10.9 %all-gather.2 = f32[8,1,256]{2,1,0:T(1,128)S(1)} all-gather(f32[1,1,256]{2,1,0:T(1,128)S(1)} %bitcast.157), channel_id=1, replica_groups=mesh['tm'=64,'state'=8] {'state'}, dimensions={0}, use_global_device_ids=true | all-gather | bytes 9216 | tf_op jit(solution)/shard_map/while/body/eval_jaxpr/all_gather | solution.py:80
  460.6 9.0 %all-gather.2 = f32[8,1,256]{2,1,0:T(1,128)S(1)} all-gather(f32[1,1,256]{2,1,0:T(1,128)S(1)} %bitcast.157), channel_id=1, replica_groups=mesh['tm'=64,'state'=8] {'state'}, dimensions={0}, use_global_device_ids=true | all-gather | bytes 9216 | tf_op jit(solution)/shard_map/while/body/eval_jaxpr/all_gather | solution.py:80
  479.9 10.9 %all-gather.2 = f32[8,1,256]{2,1,0:T(1,128)S(1)} all-gather(f32[1,1,256]{2,1,0:T(1,128)S(1)} %bitcast.157), channel_id=1, replica_groups=mesh['tm'=64,'state'=8] {'state'}, dimensions={0}, use_global_device_ids=true | all-gather | bytes 9216 | tf_op jit(solution)/shard_map/while/body/eval_jaxpr/all_gather | solution.py:80
  501.2 9.0 %all-gather.2 = f32[8,1,256]{2,1,0:T(1,128)S(1)} all-gather(f32[1,1,256]{2,1,0:T(1,128)S(1)} %bitcast.157), channel_id=1, replica_groups=mesh['tm'=64,'state'=8] {'state'}, dimensions={0}, use_global_device_ids=true | all-gather | bytes 9216 | tf_op jit(solution)/shard_map/while/body/eval_jaxpr/all_gather | solution.py:80
  520.6 10.9 %all-gather.2 = f32[8,1,256]{2,1,0:T(1,128)S(1)} all-gather(f32[1,1,256]{2,1,0:T(1,128)S(1)} %bitcast.157), channel_id=1, replica_groups=mesh['tm'=64,'state'=8] {'state'}, dimensions={0}, use_global_device_ids=true | all-gather | bytes 9216 | tf_op jit(solution)/shard_map/while/body/eval_jaxpr/all_gather | solution.py:80
  541.9 9.0 %all-gather.2 = f32[8,1,256]{2,1,0:T(1,128)S(1)} all-gather(f32[1,1,256]{2,1,0:T(1,128)S(1)} %bitcast.157), channel_id=1, replica_groups=mesh['tm'=64,'state'=8] {'state'}, dimensions={0}, use_global_device_ids=true | all-gather | bytes 9216 | tf_op jit(solution)/shard_map/while/body/eval_jaxpr/all_gather | solution.py:80
  561.2 10.9 %all-gather.2 = f32[8,1,256]{2,1,0:T(1,128)S(1)} all-gather(f32[1,1,256]{2,1,0:T(1,128)S(1)} %bitcast.157), channel_id=1, replica_groups=mesh['tm'=64,'state'=8] {'state'}, dimensions={0}, use_global_device_ids=true | all-gather | bytes 9216 | tf_op jit(solution)/shard_map/while/body/eval_jaxpr/all_gather | solution.py:80
  601.8 10.9 %all-gather.2 = f32[8,1,256]{2,1,0:T(1,128)S(1)} all-gather(f32[1,1,256]{2,1,0:T(1,128)S(1)} %bitcast.157), channel_id=1, replica_groups=mesh['tm'=64,'state'=8] {'state'}, dimensions={0}, use_global_device_ids=true | all-gather | bytes 9216 | tf_op jit(solution)/shard_map/while/body/eval_jaxpr/all_gather | solution.py:80
  642.4 10.9 %all-gather.2 = f32[8,1,256]{2,1,0:T(1,128)S(1)} all-gather(f32[1,1,256]{2,1,0:T(1,128)S(1)} %bitcast.157), channel_id=1, replica_groups=mesh['tm'=64,'state'=8] {'state'}, dimensions={0}, use_global_device_ids=true | all-gather | bytes 9216 | tf_op jit(solution)/shard_map/while/body/eval_jaxpr/all_gather | solution.py:80
  683.1 10.9 %all-gather.2 = f32[8,1,256]{2,1,0:T(1,128)S(1)} all-gather(f32[1,1,256]{2,1,0:T(1,128)S(1)} %bitcast.157), channel_id=1, replica_groups=mesh['tm'=64,'state'=8] {'state'}, dimensions={0}, use_global_device_ids=true | all-gather | bytes 9216 | tf_op jit(solution)/shard_map/while/body/eval_jaxpr/all_gather | solution.py:80
  723.7 10.9 %all-gather.2 = f32[8,1,256]{2,1,0:T(1,128)S(1)} all-gather(f32[1,1,256]{2,1,0:T(1,128)S(1)} %bitcast.157), channel_id=1, replica_groups=mesh['tm'=64,'state'=8] {'state'}, dimensions={0}, use_global_device_ids=true | all-gather | bytes 9216 | tf_op jit(solution)/shard_map/while/body/eval_jaxpr/all_gather | solution.py:80
  764.3 10.9 %all-gather.2 = f32[8,1,256]{2,1,0:T(1,128)S(1)} all-gather(f32[1,1,256]{2,1,0:T(1,128)S(1)} %bitcast.157), channel_id=1, replica_groups=mesh['tm'=64,'state'=8] {'state'}, dimensions={0}, use_global_device_ids=true | all-gather | bytes 9216 | tf_op jit(solution)/shard_map/while/body/eval_jaxpr/all_gather | solution.py:80
  804.9 10.9 %all-gather.2 = f32[8,1,256]{2,1,0:T(1,128)S(1)} all-gather(f32[1,1,256]{2,1,0:T(1,128)S(1)} %bitcast.157), channel_id=1, replica_groups=mesh['tm'=64,'state'=8] {'state'}, dimensions={0}, use_global_device_ids=true | all-gather | bytes 9216 | tf_op jit(solution)/shard_map/while/body/eval_jaxpr/all_gather | solution.py:80
  845.6 10.9 %all-gather.2 = f32[8,1,256]{2,1,0:T(1,128)S(1)} all-gather(f32[1,1,256]{2,1,0:T(1,128)S(1)} %bitcast.157), channel_id=1, replica_groups=mesh['tm'=64,'state'=8] {'state'}, dimensions={0}, use_global_device_ids=true | all-gather | bytes 9216 | tf_op jit(solution)/shard_map/while/body/eval_jaxpr/all_gather | solution.py:80
  860.1 12.7 %pmax.23 = f32[]{:T(128)} all-reduce(f32[]{:T(128)} %reduce_max.175), channel_id=1, replica_groups=mesh['tm'=64,'state'=8] {'state'}, use_global_device_ids=true, to_apply=%region_32.33 | all-reduce | flops 1 | bytes 8 | tf_op jit(solution)/shard_map/pmax | solution.py:84
  874.1 13.3 %psum.7 = f32[]{:T(128)} all-reduce(f32[]{:T(128)} %exponential_reduce_fusion.2), channel_id=1, replica_groups=mesh['tm'=64,'state'=8] {'state'}, use_global_device_ids=true, to_apply=%region_34.35 | all-reduce | flops 1 | bytes 8 | tf_op jit(solution)/shard_map/psum | solution.py:85
  (276 shorter events, 471.9 us)
Async XLA Ops:
  6.5 41.3 %all-gather.6.cloned.1.call-start = ((), (), s32[]{:S(2)}) async-start(), calls=%async_computation | async-start | bytes 1769472 | tf_op jit(solution)/shard_map/all_gather | solution.py:44
  10.8 208.6 %all-gather.8.cloned.1.call-start = ((), (), s32[]{:S(2)}) async-start(), calls=%async_computation.1 | async-start | bytes 9437184 | tf_op jit(solution)/shard_map/all_gather | solution.py:60
  93.1 51.6 %collective-permute-start.1 = (f32[2048,256]{1,0:T(8,128)}, f32[2048,256]{1,0:T(8,128)S(1)}, u32[]{:S(2)}, u32[]{:S(2)}) collective-permute-start(f32[2048,256]{1,0:T(8,128)} %fusion.4), channel_id=1, source_target_pairs={{0,8},{8,16},{16,24},{24,32},{32,40},{40,48},{48,56},{56,64},{64,7... | collective-permute-start | bytes 6291464 | tf_op jit(solution)/shard_map/ppermute | solution.py:13
  228.7 7.4 collective-permute-start
  250.2 7.3 collective-permute-start
  269.5 7.3 collective-permute-start
  290.8 7.3 collective-permute-start
  310.1 7.3 collective-permute-start
  331.4 7.3 collective-permute-start
  350.7 7.3 collective-permute-start
  372.0 7.3 collective-permute-start
  391.4 7.3 collective-permute-start
  412.7 7.3 collective-permute-start
  432.0 7.3 collective-permute-start
  453.3 7.3 collective-permute-start
  472.6 7.3 collective-permute-start
  493.9 7.3 collective-permute-start
  513.2 7.3 collective-permute-start
  534.5 7.3 collective-permute-start
  553.9 7.3 collective-permute-start
  575.2 7.3 collective-permute-start
  594.5 7.3 collective-permute-start
  615.8 7.3 collective-permute-start
  635.1 7.3 collective-permute-start
  656.4 7.3 collective-permute-start
  675.7 7.3 collective-permute-start
  737.7 7.3 collective-permute-start
  757.0 7.3 collective-permute-start
  778.3 7.3 collective-permute-start
  797.6 7.3 collective-permute-start
  818.9 7.3 collective-permute-start
  838.2 7.3 collective-permute-start
  (8 other events, 39.3 us)
Sparse Core Ops, SparseCore 0:
  10.9 36.9 all-gather.5
  159.4 59.8 all-gather.7
where the time goes:
time: 900 us; the launch traced here: 896 us
  blocking collectives  375 us (42%)
  waiting for transfers between devices  270 us (30%)
  other arithmetic  89.1 us (10%)
  starting transfers between devices  65.9 us (7%)
  matrix products  58.9 us (7%)
  local copies, waits for them, and re-layouts  21.8 us (2%)
  between operations  15 us (2%)
    all_gather x31, blocking collectives, advance(): whole_vector = lax.all_gather(incoming, 'state', axis=0, tiled=True)  309 us
    ppermute x32, waiting for transfers between devices, from_behind(): lax.ppermute(value, axis, [(source, source + steps) for source in range(i...  198 us
    ppermute x32, starting transfers between devices, from_behind(): lax.ppermute(value, axis, [(source, source + steps) for source in range(i...  65.9 us
    all_gather x1, waiting for transfers between devices, on_device(): lax.all_gather(weights, 'state', axis=1, tiled=True)  54.8 us
    dot_general x32, matrix products, apply_cols(): jnp.dot(jnp.exp(vector - vector_top)[None, :], scaled_exp, precision=lax....  29.6 us
    reduce_max x32, other arithmetic, apply_cols(): vector_top = jnp.max(vector)  22.9 us
    exp x32, other arithmetic, apply_cols(): jnp.exp(vector - vector_top)[None, :]  22.8 us
    select_n x31, other arithmetic, advance(): return jnp.where(position < 2, start_cols, apply_cols(whole_vector))  21.7 us
  transfers between devices with their start and end apart: 34, of which 34 were waited for; matrix products, arithmetic and copies ran while one was open for 1% of the time, Pallas kernels for 0%

commit v1 on v0

--- a/solution.py
+++ b/solution.py
@@ -5,6 +5,28 @@
 
 SEQS = 1
 SMOOTH = 0.001
+
+
+def in_order(blocks, dim):
+    shape = list(blocks.shape[1:])
+    shape[dim] *= blocks.shape[0]
+    return jnp.moveaxis(blocks, 0, dim).reshape(shape)
+
+
+def gather_around(x, axis, dim):
+    length = lax.axis_size(axis)
+    pairs = [(i, (i + 1) % length) for i in range(length)]
+    back = [(b, a) for a, b in pairs]
+    lower, upper = ([], [])
+    for step in range(length - 1):
+        if step % 2 == 0:
+            lower.append(lax.ppermute(lower[-1] if lower else x, axis, pairs))
+        else:
+            upper.append(lax.ppermute(upper[-1] if upper else x, axis, back))
+    parts = jnp.stack([*lower[::-1], x, *upper])
+    shift = lax.axis_index(axis) - len(lower)
+    parts = parts[(jnp.arange(length) - shift) % length]
+    return in_order(parts, dim)
 
 
 def from_behind(value, axis, steps):
@@ -57,9 +79,7 @@
     right_exp = jnp.exp(own_log - row_peak[:, None]).astype(jnp.bfloat16)
     prior_log = jax.nn.log_softmax(init_logits)
     summed = jnp.dot(
-        lax.all_gather(weights, "state", axis=1, tiled=True),
-        right_exp,
-        preferred_element_type=jnp.float32,
+        gather_around(weights, "state", 1), right_exp, preferred_element_type=jnp.float32
     )
     pair_log = left_peak[:, None] + jnp.log(summed)
     chosen = jnp.where(position == 0, own_log, pair_log)

time: 900 us -> 938 us (1.042)
  the two profiles are of different devices: /device:TPU:9 before, /device:TPU:25 now
where the time goes in v1:
time: 938 us; the launch traced here: 934 us
  blocking collectives  382 us (41%)
  waiting for transfers between devices  249 us (27%)
  other arithmetic  92.9 us (10%)
  starting transfers between devices  80.9 us (9%)
  matrix products  57.7 us (6%)
  local copies, waits for them, and re-layouts  55 us (6%)
  between operations  15 us (2%)
    all_gather x31, blocking collectives, advance(): whole_vector = lax.all_gather(incoming, 'state', axis=0, tiled=True)  315 us
    ppermute x32, waiting for transfers between devices, from_behind(): lax.ppermute(value, axis, [(source, source + steps) for source in range(i...  201 us
    ppermute x32, starting transfers between devices, from_behind(): lax.ppermute(value, axis, [(source, source + steps) for source in range(i...  62.9 us
    ppermute x4, waiting for transfers between devices, gather_around(): lower.append(lax.ppermute(lower[-1] if lower else x, axis, pairs))  31.2 us
    dot_general x32, matrix products, apply_cols(): jnp.dot(jnp.exp(vector - vector_top)[None, :], scaled_exp, precision=lax....  29.6 us
    reduce_max x32, other arithmetic, apply_cols(): vector_top = jnp.max(vector)  22.9 us
    exp x32, other arithmetic, apply_cols(): jnp.exp(vector - vector_top)[None, :]  22.8 us
    select_n x31, other arithmetic, advance(): return jnp.where(position < 2, start_cols, apply_cols(whole_vector))  21.7 us
  transfers between devices with their start and end apart: 40, of which 37 were waited for; matrix products, arithmetic and copies ran while one was open for 3% of the time, Pallas kernels for 0%

profile of v1, /device:TPU:25, one launch (start us, length us, event | category | flops | bytes accessed | tf_op | source)
XLA Modules:
  0.0 934.3 jit_solution(10042890333654069536)
XLA Ops:
  13.2 13.6 %all_gather.12 = f32[8,2048]{1,0:T(8,128)S(1)} all-gather(f32[8,256]{1,0:T(8,128)S(1)} %fusion.15), channel_id=1, replica_groups=mesh['tm'=64,'state'=8] {'state'}, dimensions={1}, use_global_device_ids=true | all-gather | bytes 73728 | tf_op jit(solution)/shard_map/all_gather | solution.py:71
  30.5 17.2 %all-gather.5.cloned.1.call-done = bf16[16,3,128,128]{3,2,1,0:T(8,128)(2,1)} async-done(((bf16[2,3,128,128]{3,2,1,0:T(8,128)(2,1)}), bf16[16,3,128,128]{3,2,1,0:T(8,128)(2,1)}) %all-gather.5.cloned.1.call-update) | async-done | bytes 1572880 | tf_op jit(solution)/shard_map/all_gather | solution.py:66
  97.4 12.8 %pmax.21 = f32[2048]{0:T(1024)S(1)} all-reduce(f32[2048]{0:T(1024)S(1)} %bitcast.187), channel_id=1, replica_groups=mesh['tm'=64,'state'=8] {'state'}, use_global_device_ids=true, to_apply=%region_24.25 | all-reduce | flops 2048 | bytes 16384 | tf_op jit(solution)/shard_map/pmax | solution.py:74
  110.3 33.6 %collective-permute-done.1 = f32[2048,256]{1,0:T(8,128)S(1)} collective-permute-done((f32[2048,256]{1,0:T(8,128)}, f32[2048,256]{1,0:T(8,128)S(1)}, u32[]{:S(2)}, u32[]{:S(2)}) %collective-permute-start.1) | collective-permute-done | bytes 2097184 | tf_op jit(solution)/shard_map/ppermute | solution.py:35
  145.7 12.9 %pmax.22 = f32[2048]{0:T(1024)S(1)} all-reduce(f32[2048]{0:T(1024)S(1)} %add_reduce_fusion), channel_id=1, replica_groups=mesh['tm'=64,'state'=8] {'state'}, use_global_device_ids=true, to_apply=%region_26.27 | all-reduce | flops 2048 | bytes 16384 | tf_op jit(solution)/shard_map/pmax | solution.py:77
  161.5 12.1 %collective-permute-done.2 = bf16[2048,256]{1,0:T(8,128)(2,1)S(1)} collective-permute-done((bf16[2048,256]{1,0:T(8,128)(2,1)}, bf16[2048,256]{1,0:T(8,128)(2,1)S(1)}, u32[]{:S(2)}, u32[]{:S(2)}) %collective-permute-start.2) | collective-permute-done | bytes 1048608 | tf_op jit(solution)/shard_map/ppermute | solution.py:23
  179.1 9.5 %collective-permute-done.3 = bf16[2048,256]{1,0:T(8,128)(2,1)S(1)} collective-permute-done((bf16[2048,256]{1,0:T(8,128)(2,1)S(1)}, bf16[2048,256]{1,0:T(8,128)(2,1)S(1)}, u32[]{:S(2)}, u32[]{:S(2)}) %collective-permute-start.3) | collective-permute-done | bytes 1048608 | tf_op jit(solution)/shard_map/ppermute | solution.py:23
  239.4 11.6 %copy.12 = bf16[2048,8,256]{0,2,1:T(8,128)(2,1)} copy(bf16[2048,8,256]{2,0,1:T(8,128)(2,1)} %bitcast.162) | data formatting | bytes 16777216 | tf_op jit(solution)/shard_map/transpose | solution.py:13
  259.1 636.9 %while.12 = (s32[]{:T(128)}, f32[256]{0:T(256)S(1)}, pred[]{:T(512)}, f32[256]{0:T(256)S(1)}, f32[2048,256]{1,0:T(8,128)S(1)}, /*index=5*/f32[256]{0:T(256)S(1)}, s32[]{:T(128)}, f32[]{:T(128)}) while((s32[]{:T(128)}, f32[256]{0:T(256)S(1)}, pred[]{:T(512)}, f32[256]{0:T(256)S(1)}, f32[2048,256]{1,0:T(8,128)S(1)}, ...), condition=%wide.region_30.31_spmd, body=%wide.region_28.30_spmd.sunk | while | flops 6296321 | bytes 2148494 | solution.py:103
  266.4 17.2 %all-gather.2 = f32[8,1,256]{2,1,0:T(1,128)S(1)} all-gather(f32[1,1,256]{2,1,0:T(1,128)S(1)} %bitcast.188), channel_id=1, replica_groups=mesh['tm'=64,'state'=8] {'state'}, dimensions={0}, use_global_device_ids=true | all-gather | bytes 9216 | tf_op jit(solution)/shard_map/while/body/eval_jaxpr/all_gather | solution.py:100
  293.9 10.9 %all-gather.2 = f32[8,1,256]{2,1,0:T(1,128)S(1)} all-gather(f32[1,1,256]{2,1,0:T(1,128)S(1)} %bitcast.188), channel_id=1, replica_groups=mesh['tm'=64,'state'=8] {'state'}, dimensions={0}, use_global_device_ids=true | all-gather | bytes 9216 | tf_op jit(solution)/shard_map/while/body/eval_jaxpr/all_gather | solution.py:100
  315.2 9.0 all-gather.2
  334.6 10.9 %all-gather.2 = f32[8,1,256]{2,1,0:T(1,128)S(1)} all-gather(f32[1,1,256]{2,1,0:T(1,128)S(1)} %bitcast.188), channel_id=1, replica_groups=mesh['tm'=64,'state'=8] {'state'}, dimensions={0}, use_global_device_ids=true | all-gather | bytes 9216 | tf_op jit(solution)/shard_map/while/body/eval_jaxpr/all_gather | solution.py:100
  355.8 9.0 all-gather.2
  375.2 10.9 %all-gather.2 = f32[8,1,256]{2,1,0:T(1,128)S(1)} all-gather(f32[1,1,256]{2,1,0:T(1,128)S(1)} %bitcast.188), channel_id=1, replica_groups=mesh['tm'=64,'state'=8] {'state'}, dimensions={0}, use_global_device_ids=true | all-gather | bytes 9216 | tf_op jit(solution)/shard_map/while/body/eval_jaxpr/all_gather | solution.py:100
  396.5 9.0 all-gather.2
  415.8 10.9 %all-gather.2 = f32[8,1,256]{2,1,0:T(1,128)S(1)} all-gather(f32[1,1,256]{2,1,0:T(1,128)S(1)} %bitcast.188), channel_id=1, replica_groups=mesh['tm'=64,'state'=8] {'state'}, dimensions={0}, use_global_device_ids=true | all-gather | bytes 9216 | tf_op jit(solution)/shard_map/while/body/eval_jaxpr/all_gather | solution.py:100
  437.1 9.0 all-gather.2
  456.4 10.9 %all-gather.2 = f32[8,1,256]{2,1,0:T(1,128)S(1)} all-gather(f32[1,1,256]{2,1,0:T(1,128)S(1)} %bitcast.188), channel_id=1, replica_groups=mesh['tm'=64,'state'=8] {'state'}, dimensions={0}, use_global_device_ids=true | all-gather | bytes 9216 | tf_op jit(solution)/shard_map/while/body/eval_jaxpr/all_gather | solution.py:100
  477.7 9.0 all-gather.2
  497.1 10.9 %all-gather.2 = f32[8,1,256]{2,1,0:T(1,128)S(1)} all-gather(f32[1,1,256]{2,1,0:T(1,128)S(1)} %bitcast.188), channel_id=1, replica_groups=mesh['tm'=64,'state'=8] {'state'}, dimensions={0}, use_global_device_ids=true | all-gather | bytes 9216 | tf_op jit(solution)/shard_map/while/body/eval_jaxpr/all_gather | solution.py:100
  537.7 10.9 %all-gather.2 = f32[8,1,256]{2,1,0:T(1,128)S(1)} all-gather(f32[1,1,256]{2,1,0:T(1,128)S(1)} %bitcast.188), channel_id=1, replica_groups=mesh['tm'=64,'state'=8] {'state'}, dimensions={0}, use_global_device_ids=true | all-gather | bytes 9216 | tf_op jit(solution)/shard_map/while/body/eval_jaxpr/all_gather | solution.py:100
  578.3 10.9 %all-gather.2 = f32[8,1,256]{2,1,0:T(1,128)S(1)} all-gather(f32[1,1,256]{2,1,0:T(1,128)S(1)} %bitcast.188), channel_id=1, replica_groups=mesh['tm'=64,'state'=8] {'state'}, dimensions={0}, use_global_device_ids=true | all-gather | bytes 9216 | tf_op jit(solution)/shard_map/while/body/eval_jaxpr/all_gather | solution.py:100
  618.9 10.9 %all-gather.2 = f32[8,1,256]{2,1,0:T(1,128)S(1)} all-gather(f32[1,1,256]{2,1,0:T(1,128)S(1)} %bitcast.188), channel_id=1, replica_groups=mesh['tm'=64,'state'=8] {'state'}, dimensions={0}, use_global_device_ids=true | all-gather | bytes 9216 | tf_op jit(solution)/shard_map/while/body/eval_jaxpr/all_gather | solution.py:100
  659.6 10.9 %all-gather.2 = f32[8,1,256]{2,1,0:T(1,128)S(1)} all-gather(f32[1,1,256]{2,1,0:T(1,128)S(1)} %bitcast.188), channel_id=1, replica_groups=mesh['tm'=64,'state'=8] {'state'}, dimensions={0}, use_global_device_ids=true | all-gather | bytes 9216 | tf_op jit(solution)/shard_map/while/body/eval_jaxpr/all_gather | solution.py:100
  700.2 10.9 %all-gather.2 = f32[8,1,256]{2,1,0:T(1,128)S(1)} all-gather(f32[1,1,256]{2,1,0:T(1,128)S(1)} %bitcast.188), channel_id=1, replica_groups=mesh['tm'=64,'state'=8] {'state'}, dimensions={0}, use_global_device_ids=true | all-gather | bytes 9216 | tf_op jit(solution)/shard_map/while/body/eval_jaxpr/all_gather | solution.py:100
  740.8 10.9 %all-gather.2 = f32[8,1,256]{2,1,0:T(1,128)S(1)} all-gather(f32[1,1,256]{2,1,0:T(1,128)S(1)} %bitcast.188), channel_id=1, replica_groups=mesh['tm'=64,'state'=8] {'state'}, dimensions={0}, use_global_device_ids=true | all-gather | bytes 9216 | tf_op jit(solution)/shard_map/while/body/eval_jaxpr/all_gather | solution.py:100
  781.4 10.9 %all-gather.2 = f32[8,1,256]{2,1,0:T(1,128)S(1)} all-gather(f32[1,1,256]{2,1,0:T(1,128)S(1)} %bitcast.188), channel_id=1, replica_groups=mesh['tm'=64,'state'=8] {'state'}, dimensions={0}, use_global_device_ids=true | all-gather | bytes 9216 | tf_op jit(solution)/shard_map/while/body/eval_jaxpr/all_gather | solution.py:100
  822.1 10.9 %all-gather.2 = f32[8,1,256]{2,1,0:T(1,128)S(1)} all-gather(f32[1,1,256]{2,1,0:T(1,128)S(1)} %bitcast.188), channel_id=1, replica_groups=mesh['tm'=64,'state'=8] {'state'}, dimensions={0}, use_global_device_ids=true | all-gather | bytes 9216 | tf_op jit(solution)/shard_map/while/body/eval_jaxpr/all_gather | solution.py:100
  862.7 10.9 %all-gather.2 = f32[8,1,256]{2,1,0:T(1,128)S(1)} all-gather(f32[1,1,256]{2,1,0:T(1,128)S(1)} %bitcast.188), channel_id=1, replica_groups=mesh['tm'=64,'state'=8] {'state'}, dimensions={0}, use_global_device_ids=true | all-gather | bytes 9216 | tf_op jit(solution)/shard_map/while/body/eval_jaxpr/all_gather | solution.py:100
  896.6 12.7 %pmax.23 = f32[]{:T(128)} all-reduce(f32[]{:T(128)} %reduce_max.175), channel_id=1, replica_groups=mesh['tm'=64,'state'=8] {'state'}, use_global_device_ids=true, to_apply=%region_32.33 | all-reduce | flops 1 | bytes 8 | tf_op jit(solution)/shard_map/pmax | solution.py:104
  910.5 14.9 %psum.7 = f32[]{:T(128)} all-reduce(f32[]{:T(128)} %exponential_reduce_fusion.2), channel_id=1, replica_groups=mesh['tm'=64,'state'=8] {'state'}, use_global_device_ids=true, to_apply=%region_34.35 | all-reduce | flops 1 | bytes 8 | tf_op jit(solution)/shard_map/psum | solution.py:105
  (314 shorter events, 541.5 us)
Async XLA Ops:
  6.5 41.2 %all-gather.5.cloned.1.call-start = ((), (), s32[]{:S(2)}) async-start(), calls=%async_computation | async-start | bytes 1769472 | tf_op jit(solution)/shard_map/all_gather | solution.py:66
  91.9 52.0 %collective-permute-start.1 = (f32[2048,256]{1,0:T(8,128)}, f32[2048,256]{1,0:T(8,128)S(1)}, u32[]{:S(2)}, u32[]{:S(2)}) collective-permute-start(f32[2048,256]{1,0:T(8,128)} %fusion.4), channel_id=1, source_target_pairs={{0,8},{8,16},{16,24},{24,32},{32,40},{40,48},{48,56},{56,64},{64,7... | collective-permute-start | bytes 6291464 | tf_op jit(solution)/shard_map/ppermute | solution.py:35
  161.5 12.1 %collective-permute-start.2 = (bf16[2048,256]{1,0:T(8,128)(2,1)}, bf16[2048,256]{1,0:T(8,128)(2,1)S(1)}, u32[]{:S(2)}, u32[]{:S(2)}) collective-permute-start(bf16[2048,256]{1,0:T(8,128)(2,1)} %exponential_convert_fusion.1), channel_id=1, source_target_pairs={{0,1},{1,2},{2,3},{3,4},{4,5},{5,6},{6,7},{7,0},{8,9},{9,10},{10,1... | collective-permute-start | bytes 3145736 | tf_op jit(solution)/shard_map/ppermute | solution.py:23
  174.5 14.1 %collective-permute-start.3 = (bf16[2048,256]{1,0:T(8,128)(2,1)S(1)}, bf16[2048,256]{1,0:T(8,128)(2,1)S(1)}, u32[]{:S(2)}, u32[]{:S(2)}) collective-permute-start(bf16[2048,256]{1,0:T(8,128)(2,1)S(1)} %collective-permute-done.2), channel_id=1, source_target_pairs={{0,1},{1,2},{2,3},{3,4},{4,5},{5,6},{6,7},{7,0},{8,9},{9,10},{10,1... | collective-permute-start | bytes 3145736 | tf_op jit(solution)/shard_map/ppermute | solution.py:23
  176.9 14.9 %collective-permute-start.6 = (bf16[2048,256]{1,0:T(8,128)(2,1)}, bf16[2048,256]{1,0:T(8,128)(2,1)}, u32[]{:S(2)}, u32[]{:S(2)}) collective-permute-start(bf16[2048,256]{1,0:T(8,128)(2,1)} %exponential_convert_fusion.1), channel_id=1, source_target_pairs={{1,0},{2,1},{3,2},{4,3},{5,4},{6,5},{7,6},{0,7},{9,8},{10,9},{11,1... | collective-permute-start | bytes 3145736 | tf_op jit(solution)/shard_map/ppermute | solution.py:25
  188.6 14.2 %collective-permute-start.4 = (bf16[2048,256]{1,0:T(8,128)(2,1)S(1)}, bf16[2048,256]{1,0:T(8,128)(2,1)}, u32[]{:S(2)}, u32[]{:S(2)}) collective-permute-start(bf16[2048,256]{1,0:T(8,128)(2,1)S(1)} %collective-permute-done.3), channel_id=1, source_target_pairs={{0,1},{1,2},{2,3},{3,4},{4,5},{5,6},{6,7},{7,0},{8,9},{9,10},{10,1... | collective-permute-start | bytes 3145736 | tf_op jit(solution)/shard_map/ppermute | solution.py:23
  191.8 18.8 %collective-permute-start.7 = (bf16[2048,256]{1,0:T(8,128)(2,1)}, bf16[2048,256]{1,0:T(8,128)(2,1)}, u32[]{:S(2)}, u32[]{:S(2)}) collective-permute-start(bf16[2048,256]{1,0:T(8,128)(2,1)} %collective-permute-done.6), channel_id=1, source_target_pairs={{1,0},{2,1},{3,2},{4,3},{5,4},{6,5},{7,6},{0,7},{9,8},{10,9},{11,1... | collective-permute-start | bytes 3145736 | tf_op jit(solution)/shard_map/ppermute | solution.py:25
  202.8 14.6 %collective-permute-start.5 = (bf16[2048,256]{1,0:T(8,128)(2,1)}, bf16[2048,256]{1,0:T(8,128)(2,1)}, u32[]{:S(2)}, u32[]{:S(2)}) collective-permute-start(bf16[2048,256]{1,0:T(8,128)(2,1)} %collective-permute-done.4), channel_id=1, source_target_pairs={{0,1},{1,2},{2,3},{3,4},{4,5},{5,6},{6,7},{7,0},{8,9},{9,10},{10,1... | collective-permute-start | bytes 3145736 | tf_op jit(solution)/shard_map/ppermute | solution.py:23
  210.6 19.6 %collective-permute-start.8 = (bf16[2048,256]{1,0:T(8,128)(2,1)}, bf16[2048,256]{1,0:T(8,128)(2,1)S(1)}, u32[]{:S(2)}, u32[]{:S(2)}) collective-permute-start(bf16[2048,256]{1,0:T(8,128)(2,1)} %collective-permute-done.7), channel_id=1, source_target_pairs={{1,0},{2,1},{3,2},{4,3},{5,4},{6,5},{7,6},{0,7},{9,8},{10,9},{11,1... | collective-permute-start | bytes 3145736 | tf_op jit(solution)/shard_map/ppermute | solution.py:25
  259.1 7.3 collective-permute-start
  286.6 7.3 collective-permute-start
  307.9 7.3 collective-permute-start
  327.2 7.3 collective-permute-start
  348.5 7.3 collective-permute-start
  367.9 7.3 collective-permute-start
  389.1 7.3 collective-permute-start
  408.5 7.3 collective-permute-start
  429.8 7.3 collective-permute-start
  449.1 7.3 collective-permute-start
  470.4 7.3 collective-permute-start
  489.7 7.3 collective-permute-start
  511.0 7.3 collective-permute-start
  530.4 7.3 collective-permute-start
  551.6 7.3 collective-permute-start
  571.0 7.3 collective-permute-start
  592.3 7.3 collective-permute-start
  611.6 7.3 collective-permute-start
  673.5 7.3 collective-permute-start
  692.9 7.3 collective-permute-start
  714.1 7.3 collective-permute-start
  733.5 7.3 collective-permute-start
  754.8 7.3 collective-permute-start
  (21 other events, 233.1 us)
Sparse Core Ops, SparseCore 0:
  10.9 36.7 all-gather.4
